TPU v7x, 256 devices: a whole 4x4x8 slice. The times are simulated.
256 devices in a mesh: dp: 32 (over y, x, core), filter: 8 (over z).
Axes of the slice: x: 4, y: 4, z: 8, core: 2. Of those that a mesh axis runs over, the one named last changes fastest.
Arguments:
- inputs: bfloat16 [32, 48, 24, 1024], P('dp', None, None, 'filter'), may hold values from -6 to 6
- kernel: bfloat16 [3, 3, 1024, 1024], P(None, None, 'filter'), may hold values from -0.0625 to 0.0625
- cotangent: bfloat16 [32, 48, 24, 1024], P('dp', 'filter'), may hold values from -6 to 6
Outputs:
- outputs: bfloat16 [32, 48, 24, 1024], P('dp', 'filter')
- input_grad: bfloat16 [32, 48, 24, 1024], P('dp', None, None, 'filter')
- kernel_grad: float32 [1024, 3, 3, 1024], P('dp', None, None, 'filter')
All inputs are finite; a program needn't handle non-finite values.
Results may differ from a plain program's by a relative error of at most 0.001.
Values may be sent and summed in bfloat16 or wider, within the bound.
No kernel may reach another device: no remote copies, remote signals or barrier semaphores. Data moves between devices by JAX's collectives and lax.ppermute only.
A program may use at most 128 MiB of HBM per device.

v0:
```python
import jax
import jax.numpy as jnp
from jax import lax
from jax.sharding import PartitionSpec as P


def conv_rows(xpad, weights, count, width):
    total = jnp.zeros((count, width, weights.shape[3]), jnp.float32)
    for a in range(3):
        for b in range(3):
            total = total + jnp.einsum(
                "hwi,io->hwo",
                xpad[a : a + count, b : b + width],
                weights[a, b],
                preferred_element_type=jnp.float32,
            )
    return total


def on_device(inputs, kernel, cotangent):
    sample = inputs[0]
    height = sample.shape[0]
    width = sample.shape[1]
    local_in = sample.shape[2]
    channels = kernel.shape[3]
    groups = lax.axis_size("filter")
    my_rows = height // groups
    xpad = jnp.pad(sample, ((1, 1), (1, 1), (0, 0)))
    summed = lax.psum_scatter(
        conv_rows(xpad, kernel, my_rows * lax.axis_size("filter"), width),
        "filter",
        scatter_dimension=0,
        tiled=True,
    )
    outputs = summed.astype(jnp.bfloat16)[None]
    start = jnp.int32(0)
    back_pad = jnp.zeros((height + 2, width + 2, local_in), jnp.float32)
    grad_rows = lax.all_gather(cotangent, "filter", axis=1, tiled=True)[0]
    count = grad_rows.shape[0]
    taps = []
    for a in range(3):
        for b in range(3):
            contrib = jnp.einsum(
                "hwo,io->hwi", grad_rows, kernel[a, b], preferred_element_type=jnp.float32
            )
            region = lax.dynamic_slice(back_pad, (start + a, b, 0), (count, width, local_in))
            back_pad = lax.dynamic_update_slice(back_pad, region + contrib, (start + a, b, 0))
            taps.append(
                jnp.einsum(
                    "hwi,hwo->oi",
                    xpad[a : a + count, b : b + width],
                    grad_rows,
                    preferred_element_type=jnp.float32,
                )
            )
    grads = jnp.stack(taps, 1).reshape(channels, 3, 3, local_in)
    back_pad, grads = (back_pad, grads)
    input_grad = back_pad[1:-1, 1:-1].astype(jnp.bfloat16)[None]
    samples = lax.axis_size("dp")
    scale = 1.0 / jnp.sqrt(jnp.float32(samples * height * width))
    whole = lax.psum(grads, "dp")
    share = channels // samples
    mine = lax.dynamic_slice_in_dim(whole, lax.axis_index("dp") * share, share, 0)
    return (outputs, input_grad, mine * scale)


def solution(mesh):
    return jax.shard_map(
        on_device,
        mesh=mesh,
        in_specs=(
            P("dp", None, None, "filter"),
            P(None, None, "filter", None),
            P("dp", "filter", None, None),
        ),
        out_specs=(
            P("dp", "filter", None, None),
            P("dp", None, None, "filter"),
            P("dp", None, None, "filter"),
        ),
        check_vma=False,
    )
```

profile of v0, /device:TPU:1, one launch (start us, length us, event | category | flops | bytes accessed | tf_op | source)
XLA Modules:
  0.0 268.3 jit_solution(1624768555959365311)
XLA Ops:
  7.2 0.0 all-gather.2.cloned.1.call-start
  7.2 0.7 all-gather.2.cloned.1.call-update
  7.9 0.0 all-reduce.4.cloned.1.call-start
  7.9 0.0 copy-start.1
  8.0 4.1 %fusion.124 = f32[48,24,1024]{2,1,0:T(8,128)} fusion(bf16[3,3,128,1024]{3,2,1,0:T(8,128)(2,1)} %param.4, bf16[48,24,128]{2,1,0:T(8,128)(2,1)} %bitcast.236), kind=kOutput, calls=%fused_computation.79 | convolution fusion | flops 301989888 | bytes 5275648 | tf_op jit(solution)/shard_map/hwi,io->hwo/dot_general | solution.py:11
  12.0 0.0 copy-done.1
  12.0 3.8 %fusion.127 = f32[48,24,1024]{2,1,0:T(8,128)} fusion(bf16[3,3,128,1024]{3,2,1,0:T(8,128)(2,1)} %param.4, bf16[48,24,128]{2,1,0:T(8,128)(2,1)S(1)} %bitcast.237), kind=kOutput, calls=%fused_computation.82 | convolution fusion | flops 301989888 | bytes 5275648 | tf_op jit(solution)/shard_map/hwi,io->hwo/dot_general | solution.py:11
  15.8 3.9 %fusion.130 = f32[48,24,1024]{2,1,0:T(8,128)} fusion(bf16[3,3,128,1024]{3,2,1,0:T(8,128)(2,1)} %param.4, bf16[48,24,128]{2,1,0:T(8,128)(2,1)S(1)} %bitcast.238), kind=kOutput, calls=%fused_computation.85 | convolution fusion | flops 301989888 | bytes 5275648 | tf_op jit(solution)/shard_map/hwi,io->hwo/dot_general | solution.py:11
  19.8 3.9 %fusion.136 = f32[48,24,1024]{2,1,0:T(8,128)} fusion(bf16[3,3,128,1024]{3,2,1,0:T(8,128)(2,1)} %param.4, bf16[48,24,128]{2,1,0:T(8,128)(2,1)S(1)} %bitcast.239), kind=kOutput, calls=%fused_computation.91 | convolution fusion | flops 301989888 | bytes 5275648 | tf_op jit(solution)/shard_map/hwi,io->hwo/dot_general | solution.py:11
  23.6 3.9 %fusion.139 = f32[48,24,1024]{2,1,0:T(8,128)} fusion(bf16[3,3,128,1024]{3,2,1,0:T(8,128)(2,1)} %param.4, bf16[48,24,128]{2,1,0:T(8,128)(2,1)S(1)} %bitcast.240), kind=kOutput, calls=%fused_computation.94 | convolution fusion | flops 301989888 | bytes 5275648 | tf_op jit(solution)/shard_map/hwi,io->hwo/dot_general | solution.py:11
  27.5 24.7 %all-gather.2.cloned.1.call-done = bf16[1,48,24,1024]{3,2,0,1:T(8,128)(2,1)} async-done(((bf16[1,6,24,1024]{3,2,0,1:T(8,128)(2,1)}), bf16[1,48,24,1024]{3,2,0,1:T(8,128)(2,1)}) %all-gather.2.cloned.1.call-update) | async-done | bytes 2359312 | tf_op jit(solution)/shard_map/all_gather | solution.py:38
  52.3 0.0 copy-start
  52.3 3.2 %fusion.69 = f32[1024,9,128]{0,2,1:T(8,128)} fusion(bf16[1,48,24,1024]{3,2,0,1:T(8,128)(2,1)} %all-gather.2.cloned.1.call-done, bf16[48,24,128]{2,1,0:T(8,128)(2,1)S(1)} %bitcast.241), kind=kOutput, calls=%fused_computation.48 | convolution fusion | flops 301989888 | bytes 3178496 | tf_op jit(solution)/shard_map/hwi,hwo->oi/dot_general | solution.py:49
  55.4 0.0 copy-done
  55.4 1.3 fusion.75
  56.8 1.4 fusion.81
  58.1 1.4 fusion.87
  59.5 1.4 fusion.93
  60.9 1.3 fusion.99
  62.2 1.3 fusion.105
  63.5 1.4 fusion.111
  64.9 1.4 fusion.117
  66.3 6.0 %copy.46 = f32[1024,3,3,128]{3,0,2,1:T(8,128)} copy(f32[1024,3,3,128]{0,3,2,1:T(8,128)} %bitcast.58) | data formatting | bytes 9437184 | tf_op jit(solution)/shard_map/reshape | solution.py:56
  72.3 0.0 all-reduce.4.cloned.1.call-update
  72.3 0.0 reduce-scatter.2.cloned.1.call-start
  72.4 0.0 slice-start
  72.4 0.0 slice-start.2
  72.4 4.2 %fusion.145 = f32[48,24,1024]{2,1,0:T(8,128)} fusion(bf16[3,3,128,1024]{3,2,1,0:T(8,128)(2,1)} %param.4, bf16[48,24,128]{2,1,0:T(8,128)(2,1)S(1)} %bitcast.249), kind=kOutput, calls=%fused_computation.100 | convolution fusion | flops 301989888 | bytes 5275648 | tf_op jit(solution)/shard_map/hwi,io->hwo/dot_general | solution.py:11
  76.6 0.0 slice-start.1
  76.6 0.0 slice-start.3
  76.6 4.0 %fusion.142 = f32[48,24,1024]{2,1,0:T(8,128)} fusion(bf16[3,3,128,1024]{3,2,1,0:T(8,128)(2,1)} %param.4, bf16[48,24,128]{2,1,0:T(8,128)(2,1)S(1)} %bitcast.250), kind=kOutput, calls=%fused_computation.97 | convolution fusion | flops 301989888 | bytes 5275648 | tf_op jit(solution)/shard_map/hwi,io->hwo/dot_general | solution.py:11
  80.6 3.9 %fusion.133 = f32[48,24,1024]{2,1,0:T(8,128)} fusion(bf16[3,3,128,1024]{3,2,1,0:T(8,128)(2,1)} %param.4, bf16[1,48,24,128]{3,2,1,0:T(8,128)(2,1)S(1)} %copy-done.1), kind=kOutput, calls=%fused_computation.88 | convolution fusion | flops 301989888 | bytes 5275648 | tf_op jit(solution)/shard_map/hwi,io->hwo/dot_general | solution.py:11
  84.6 0.0 slice-done
  84.6 0.0 slice-done.2
  84.6 0.0 slice-done.1
  84.6 0.0 slice-done.3
  84.6 13.1 %add_add_fusion = f32[48,24,1024]{2,1,0:T(8,128)} fusion(f32[48,24,1024]{2,1,0:T(8,128)S(1)} %bitcast.253, f32[48,24,1024]{2,1,0:T(8,128)S(1)} %bitcast.255, f32[48,24,1024]{2,1,0:T(8,128)} %fusion.130, f32[48,24,1024]{2,1,0:T(8,128)} %fusion.133, f32[48,24,1024]{2,1,0:T(8,128)} %fusion.136, f32[48,24,1024]{2,1,0:T(8,128)} %fusion.139, ...), kind=kOutput, calls=%fused_computation | convolution fusion | flops 311427072 | bytes 43024384 | tf_op jit(solution)/shard_map/hwi,io->hwo/dot_general | solution.py:11
  97.7 0.0 reduce-scatter.2.cloned.1.call-update
  97.7 1.7 fusion.34
  99.5 0.1 dynamic_update_slice.27
  99.6 2.6 fusion.36
  102.1 6.3 %dynamic_update_slice.28 = f32[50,26,128]{2,1,0:T(8,128)S(1)} dynamic-update-slice(f32[50,26,128]{2,1,0:T(8,128)S(1)} %dynamic_update_slice.27, f32[48,24,128]{2,1,0:T(8,128)} %fusion.36, s32[]{:T(128)} %constant.5.clone.1, s32[]{:T(128)} %constant.6.clone.1, s32[]{:T(128)} %constant.5.clone.1) | dynamic-update-slice | bytes 1179652 | tf_op jit(solution)/shard_map/dynamic_update_slice | solution.py:47
  108.5 2.6 fusion.39
  111.0 6.3 %dynamic_update_slice.29 = f32[50,26,128]{2,1,0:T(8,128)S(1)} dynamic-update-slice(f32[50,26,128]{2,1,0:T(8,128)S(1)} %dynamic_update_slice.28, f32[48,24,128]{2,1,0:T(8,128)} %fusion.39, s32[]{:T(128)} %constant.5.clone.1, s32[]{:T(128)} %constant.7.clone.1, s32[]{:T(128)} %constant.5.clone.1) | dynamic-update-slice | bytes 1179652 | tf_op jit(solution)/shard_map/dynamic_update_slice | solution.py:47
  117.3 1.9 fusion.45
  119.2 2.6 fusion.48
  121.8 6.3 %dynamic_update_slice.31 = f32[50,26,128]{2,1,0:T(8,128)S(1)} dynamic-update-slice(f32[50,26,128]{2,1,0:T(8,128)S(1)} %fusion.45, f32[48,24,128]{2,1,0:T(8,128)} %fusion.48, s32[]{:T(128)} %constant.6.clone.1, s32[]{:T(128)} %constant.6.clone.1, s32[]{:T(128)} %constant.5.clone.1) | dynamic-update-slice | bytes 1179652 | tf_op jit(solution)/shard_map/dynamic_update_slice | solution.py:47
  128.1 2.6 fusion.51
  130.6 6.3 %dynamic_update_slice.32 = f32[50,26,128]{2,1,0:T(8,128)S(1)} dynamic-update-slice(f32[50,26,128]{2,1,0:T(8,128)S(1)} %dynamic_update_slice.31, f32[48,24,128]{2,1,0:T(8,128)} %fusion.51, s32[]{:T(128)} %constant.6.clone.1, s32[]{:T(128)} %constant.7.clone.1, s32[]{:T(128)} %constant.5.clone.1) | dynamic-update-slice | bytes 1179652 | tf_op jit(solution)/shard_map/dynamic_update_slice | solution.py:47
  136.9 1.8 fusion.57
  138.8 2.6 fusion.60
  141.3 6.2 %dynamic_update_slice.34 = f32[50,26,128]{2,1,0:T(8,128)S(1)} dynamic-update-slice(f32[50,26,128]{2,1,0:T(8,128)S(1)} %fusion.57, f32[48,24,128]{2,1,0:T(8,128)} %fusion.60, s32[]{:T(128)} %constant.7.clone.1, s32[]{:T(128)} %constant.6.clone.1, s32[]{:T(128)} %constant.5.clone.1) | dynamic-update-slice | bytes 1179652 | tf_op jit(solution)/shard_map/dynamic_update_slice | solution.py:47
  147.6 2.6 fusion.63
  150.1 6.2 %dynamic_update_slice.35 = f32[50,26,128]{2,1,0:T(8,128)S(1)} dynamic-update-slice(f32[50,26,128]{2,1,0:T(8,128)S(1)} %dynamic_update_slice.34, f32[48,24,128]{2,1,0:T(8,128)} %fusion.63, s32[]{:T(128)} %constant.7.clone.1, s32[]{:T(128)} %constant.7.clone.1, s32[]{:T(128)} %constant.5.clone.1) | dynamic-update-slice | bytes 1179652 | tf_op jit(solution)/shard_map/dynamic_update_slice | solution.py:47
  156.4 0.8 fusion.120
  157.1 40.0 %all-reduce.4.cloned.1.call-done = f32[1024,3,3,128]{3,0,2,1:T(8,128)} async-done(((f32[1024,3,3,128]{3,0,2,1:T(8,128)}), f32[1024,3,3,128]{3,0,2,1:T(8,128)}) %all-reduce.4.cloned.1.call-update) | async-done | bytes 4718608 | tf_op jit(solution)/shard_map/psum | solution.py:61
  197.2 1.6 dynamic-slice_multiply_fusion
  198.8 61.2 %reduce-scatter.2.cloned.1.call-done = f32[6,24,1024]{2,1,0:T(8,128)} async-done(((f32[48,24,1024]{2,1,0:T(8,128)}), f32[6,24,1024]{2,1,0:T(8,128)}) %reduce-scatter.2.cloned.1.call-update) | async-done | bytes 589840 | tf_op jit(solution)/shard_map/reduce_scatter | solution.py:29
  259.9 1.8 convert_bitcast_fusion
  (2 shorter events, 0.0 us)
Async XLA Ops:
  7.2 45.1 %all-gather.2.cloned.1.call-start = ((), (), s32[]{:S(2)}) async-start(), calls=%async_computation.2 | async-start | bytes 2654208 | tf_op jit(solution)/shard_map/all_gather | solution.py:38
  7.9 189.3 %all-reduce.4.cloned.1.call-start = ((), (), s32[]{:S(2)}) async-start(), calls=%async_computation.3 | async-start | bytes 9437184 | tf_op jit(solution)/shard_map/psum | solution.py:61
  7.9 4.1 %copy-start.1 = (bf16[1,48,24,128]{3,2,1,0:T(8,128)(2,1)S(1)}, bf16[1,48,24,128]{3,2,1,0:T(8,128)(2,1)}, u32[]{:S(2)}) copy-start(bf16[1,48,24,128]{3,2,1,0:T(8,128)(2,1)} %param.3) | copy-start | bytes 884740
  52.3 3.2 %copy-start = (bf16[1,48,24,1024]{3,2,0,1:T(8,128)(2,1)S(1)}, bf16[1,48,24,1024]{3,2,0,1:T(8,128)(2,1)}, u32[]{:S(2)}) copy-start(bf16[1,48,24,1024]{3,2,0,1:T(8,128)(2,1)} %all-gather.2.cloned.1.call-done) | copy-start | bytes 7077892
  72.3 187.6 %reduce-scatter.2.cloned.1.call-start = ((), (), s32[]{:S(2)}) async-start(), calls=%async_computation.1 | async-start | bytes 5308416 | tf_op jit(solution)/shard_map/reduce_scatter | solution.py:29
  72.4 12.2 %slice-start = ((s8[4718592]{0:T(1024)(128)(4,1)}), s8[4194304]{0:T(1024)(128)(4,1)S(1)}, s32[]{:S(2)}) async-start(s8[4718592]{0:T(1024)(128)(4,1)} %bitcast.252), calls=%async_computation.4 | async-start | bytes 8388608
  72.4 12.2 %slice-start.2 = ((s8[4718592]{0:T(1024)(128)(4,1)}), s8[4194304]{0:T(1024)(128)(4,1)S(1)}, s32[]{:S(2)}) async-start(s8[4718592]{0:T(1024)(128)(4,1)} %bitcast.254), calls=%async_computation.6 | async-start | bytes 8388608
  76.6 8.0 %slice-start.1 = ((s8[4718592]{0:T(1024)(128)(4,1)}), s8[524288]{0:T(1024)(128)(4,1)S(1)}, s32[]{:S(2)}) async-start(s8[4718592]{0:T(1024)(128)(4,1)} %bitcast.252), calls=%async_computation.5 | async-start | bytes 1048576
  76.6 8.0 %slice-start.3 = ((s8[4718592]{0:T(1024)(128)(4,1)}), s8[524288]{0:T(1024)(128)(4,1)S(1)}, s32[]{:S(2)}) async-start(s8[4718592]{0:T(1024)(128)(4,1)} %bitcast.254), calls=%async_computation.7 | async-start | bytes 1048576
Sparse Core Ops, SparseCore 0:
  9.8 42.4 all-gather.1
  72.5 124.6 all-reduce.3
  199.9 59.9 reduce-scatter.1
where the time goes:
time: 270 us; the launch traced here: 268 us
  waiting for transfers between devices  127 us (47%)
  matrix products  79.7 us (30%)
  local copies, waits for them, and re-layouts  44.6 us (17%)
  between operations  13.9 us (5%)
  other arithmetic  3.4 us (1%)
    reduce_scatter x1, waiting for transfers between devices, on_device(): lax.psum_scatter(conv_rows(xpad, kernel, my_rows * lax.axis_size('filter'...  61.2 us
    dot_general x9, matrix products, conv_rows(): jnp.einsum('hwi,io->hwo', xpad[a:a + count, b:b + width], weights[a, b],...  44.8 us
    psum x1, waiting for transfers between devices, on_device(): whole = lax.psum(grads, 'dp')  40 us
    dynamic_update_slice x7, local copies, waits for them, and re-layouts, on_device(): lax.dynamic_update_slice(back_pad, region + contrib, (start + a, b, 0))  37.7 us
    all_gather x1, waiting for transfers between devices, on_device(): grad_rows = lax.all_gather(cotangent, 'filter', axis=1, tiled=True)[0]  24.7 us
    dot_general x9, matrix products, on_device(): jnp.einsum('hwo,io->hwi', grad_rows, kernel[a, b], preferred_element_type...  20.9 us
    dot_general x9, matrix products, on_device(): jnp.einsum('hwi,hwo->oi', xpad[a:a + count, b:b + width], grad_rows, pref...  14 us
    reshape x1, local copies, waits for them, and re-layouts, on_device(): grads = jnp.stack(taps, 1).reshape(channels, 3, 3, local_in)  6.04 us
  transfers between devices with their start and end apart: 3, of which 3 were waited for; matrix products, arithmetic and copies ran while one was open for 39% of the time, Pallas kernels for 0%

commit v1 on v0

--- a/solution.py
+++ b/solution.py
@@ -1,7 +1,22 @@
+import functools
 import jax
 import jax.numpy as jnp
 from jax import lax
 from jax.sharding import PartitionSpec as P
+
+
+def slots_make(xin, mesh_dim):
+    num_devices = lax.axis_size(mesh_dim)
+    raw_out = xin
+    for pp in [jj for jj in (1, 2, 4, 8, 16) if jj < num_devices]:
+        block_last = lax.ppermute(
+            raw_out, axis_name=mesh_dim, perm=[(w, w ^ pp) for w in range(num_devices)]
+        )
+        raw_out = raw_out + block_last
+    return raw_out
+
+
+pair_domain = functools.partial(slots_make, mesh_dim="dp")
 
 
 def conv_rows(xpad, weights, count, width):
@@ -58,7 +73,7 @@
     input_grad = back_pad[1:-1, 1:-1].astype(jnp.bfloat16)[None]
     samples = lax.axis_size("dp")
     scale = 1.0 / jnp.sqrt(jnp.float32(samples * height * width))
-    whole = lax.psum(grads, "dp")
+    whole = pair_domain(grads)
     share = channels // samples
     mine = lax.dynamic_slice_in_dim(whole, lax.axis_index("dp") * share, share, 0)
     return (outputs, input_grad, mine * scale)

time: 270 us -> 519 us (1.92)
  waiting for transfers between devices: 127 us -> 362 us
  matrix products: 79.7 us -> 66.8 us
  other arithmetic: 3.4 us -> 16 us
  starting transfers between devices: 0.12 us -> 11.8 us
    ppermute x0 -> x5, waiting for transfers between devices: none -> 317 us  [slots_make(): lax.ppermute(raw_out, axis_name=mesh_dim, perm=[(w, w ^ pp) for w in rang...]
    reduce_scatter x1, waiting for transfers between devices: 61.2 us -> 0.01 us  [on_device(): lax.psum_scatter(conv_rows(xpad, kernel, my_rows * lax.axis_size('filter'...]
    psum x1 -> x0, waiting for transfers between devices: 40 us -> none  [on_device(): whole = lax.psum(grads, 'dp')]
    all_gather x1, waiting for transfers between devices: 24.7 us -> 44.3 us  [on_device(): grad_rows = lax.all_gather(cotangent, 'filter', axis=1, tiled=True)[0]]
    dot_general x9, matrix products: 44.8 us -> 31.8 us  [conv_rows(): jnp.einsum('hwi,io->hwo', xpad[a:a + count, b:b + width], weights[a, b],...]
    add x0 -> x4, other arithmetic: none -> 12.6 us  [slots_make(): raw_out = raw_out + block_last]
    ppermute x0 -> x5, starting transfers between devices: none -> 11.7 us  [slots_make(): lax.ppermute(raw_out, axis_name=mesh_dim, perm=[(w, w ^ pp) for w in rang...]
  transfers between devices with their start and end apart: 3 -> 7, of which waited for: 3 -> 6; matrix products, arithmetic and copies ran while one was open for 39% -> 19% of each run, Pallas kernels for 0% -> 0%
where the time goes in v1:
time: 519 us; the launch traced here: 515 us
  waiting for transfers between devices  362 us (70%)
  matrix products  66.8 us (13%)
  local copies, waits for them, and re-layouts  44.6 us (9%)
  other arithmetic  16 us (3%)
  between operations  14.2 us (3%)
  starting transfers between devices  11.8 us (2%)
    ppermute x5, waiting for transfers between devices, slots_make(): lax.ppermute(raw_out, axis_name=mesh_dim, perm=[(w, w ^ pp) for w in rang...  317 us
    all_gather x1, waiting for transfers between devices, on_device(): grad_rows = lax.all_gather(cotangent, 'filter', axis=1, tiled=True)[0]  44.3 us
    dynamic_update_slice x7, local copies, waits for them, and re-layouts, on_device(): lax.dynamic_update_slice(back_pad, region + contrib, (start + a, b, 0))  37.7 us
    dot_general x9, matrix products, conv_rows(): jnp.einsum('hwi,io->hwo', xpad[a:a + count, b:b + width], weights[a, b],...  31.8 us
    dot_general x9, matrix products, on_device(): jnp.einsum('hwo,io->hwi', grad_rows, kernel[a, b], preferred_element_type...  21 us
    dot_general x9, matrix products, on_device(): jnp.einsum('hwi,hwo->oi', xpad[a:a + count, b:b + width], grad_rows, pref...  14 us
    add x4, other arithmetic, slots_make(): raw_out = raw_out + block_last  12.6 us
    ppermute x5, starting transfers between devices, slots_make(): lax.ppermute(raw_out, axis_name=mesh_dim, perm=[(w, w ^ pp) for w in rang...  11.7 us
  transfers between devices with their start and end apart: 7, of which 6 were waited for; matrix products, arithmetic and copies ran while one was open for 19% of the time, Pallas kernels for 0%

profile of v1, /device:TPU:1, one launch (start us, length us, event | category | flops | bytes accessed | tf_op | source)
XLA Modules:
  0.0 515.2 jit_solution(9559041117039875025)
XLA Ops:
  7.2 0.0 copy-start.1
  7.2 0.0 all-gather.2.cloned.1.call-start
  7.2 0.7 all-gather.2.cloned.1.call-update
  7.9 0.0 reduce-scatter.2.cloned.1.call-start
  8.0 44.3 %all-gather.2.cloned.1.call-done = bf16[1,48,24,1024]{3,2,0,1:T(8,128)(2,1)} async-done(((bf16[1,6,24,1024]{3,2,0,1:T(8,128)(2,1)}), bf16[1,48,24,1024]{3,2,0,1:T(8,128)(2,1)}) %all-gather.2.cloned.1.call-update) | async-done | bytes 2359312 | tf_op jit(solution)/shard_map/all_gather | solution.py:53
  52.3 0.0 copy-start
  52.3 3.2 fusion.69
  55.5 0.0 copy-done.1
  55.5 0.0 copy-done
  55.5 1.3 fusion.75
  56.8 1.4 fusion.81
  58.2 1.3 fusion.87
  59.5 1.4 fusion.93
  60.9 1.3 fusion.99
  62.2 1.4 fusion.105
  63.6 1.3 fusion.111
  64.9 1.3 fusion.117
  66.3 6.1 %copy.48 = f32[1024,3,3,128]{3,0,2,1:T(8,128)} copy(f32[1024,3,3,128]{0,3,2,1:T(8,128)} %bitcast.58) | data formatting | bytes 9437184 | tf_op jit(solution)/shard_map/reshape | solution.py:71
  72.4 3.6 collective-permute-start
  76.0 7.7 %collective-permute-done = f32[1024,3,3,128]{3,0,2,1:T(8,128)S(1)} collective-permute-done((f32[1024,3,3,128]{3,0,2,1:T(8,128)}, f32[1024,3,3,128]{3,0,2,1:T(8,128)S(1)}, u32[]{:S(2)}, u32[]{:S(2)}) %collective-permute-start) | collective-permute-done | bytes 4718624 | tf_op jit(solution)/shard_map/ppermute | solution.py:12
  83.8 3.1 add.88
  86.9 0.0 copy-start.2
  86.9 1.3 collective-permute-start.1
  88.1 101.8 %collective-permute-done.1 = f32[1024,3,3,128]{3,0,2,1:T(8,128)S(1)} collective-permute-done((f32[1024,3,3,128]{3,0,2,1:T(8,128)S(1)}, f32[1024,3,3,128]{3,0,2,1:T(8,128)S(1)}, u32[]{:S(2)}, u32[]{:S(2)}) %collective-permute-start.1) | collective-permute-done | bytes 4718624 | tf_op jit(solution)/shard_map/ppermute | solution.py:12
  190.0 2.6 add.89
  192.6 2.7 collective-permute-start.2
  195.3 0.0 copy-done.2
  195.3 0.8 fusion.124
  196.1 0.8 fusion.127
  196.9 3.0 fusion.130
  199.9 2.9 fusion.136
  202.7 3.0 fusion.139
  205.7 3.0 fusion.145
  208.7 2.9 fusion.142
  211.6 3.0 fusion.133
  214.6 12.5 %add_add_fusion = f32[48,24,1024]{2,1,0:T(8,128)} fusion(f32[48,24,1024]{2,1,0:T(8,128)S(1)} %fusion.124, f32[48,24,1024]{2,1,0:T(8,128)S(1)} %fusion.127, f32[48,24,1024]{2,1,0:T(8,128)} %fusion.130, f32[48,24,1024]{2,1,0:T(8,128)} %fusion.133, f32[48,24,1024]{2,1,0:T(8,128)} %fusion.136, f32[48,24,1024]{2,1,0:T(8,128)} %fusion.139, ...), kind=kOutput, calls=%fused_computation | convolution fusion | flops 311427072 | bytes 43024384 | tf_op jit(solution)/shard_map/hwi,io->hwo/dot_general | solution.py:26
  227.1 0.0 reduce-scatter.2.cloned.1.call-update
  227.1 69.4 %collective-permute-done.2 = f32[1024,3,3,128]{3,0,2,1:T(8,128)} collective-permute-done((f32[1024,3,3,128]{3,0,2,1:T(8,128)}, f32[1024,3,3,128]{3,0,2,1:T(8,128)}, u32[]{:S(2)}, u32[]{:S(2)}) %collective-permute-start.2) | collective-permute-done | bytes 4718624 | tf_op jit(solution)/shard_map/ppermute | solution.py:12
  296.5 4.3 add.90
  300.8 1.4 collective-permute-start.3
  302.2 99.9 %collective-permute-done.3 = f32[1024,3,3,128]{3,0,2,1:T(8,128)S(1)} collective-permute-done((f32[1024,3,3,128]{3,0,2,1:T(8,128)S(1)}, f32[1024,3,3,128]{3,0,2,1:T(8,128)S(1)}, u32[]{:S(2)}, u32[]{:S(2)}) %collective-permute-start.3) | collective-permute-done | bytes 4718624 | tf_op jit(solution)/shard_map/ppermute | solution.py:12
  402.0 2.6 add.91
  404.7 2.7 collective-permute-start.4
  407.4 1.7 fusion.34
  409.1 0.1 dynamic_update_slice.27
  409.2 2.6 fusion.36
  411.8 6.3 %dynamic_update_slice.28 = f32[50,26,128]{2,1,0:T(8,128)S(1)} dynamic-update-slice(f32[50,26,128]{2,1,0:T(8,128)S(1)} %dynamic_update_slice.27, f32[48,24,128]{2,1,0:T(8,128)} %fusion.36, s32[]{:T(128)} %constant.5.clone.1, s32[]{:T(128)} %constant.6.clone.1, s32[]{:T(128)} %constant.5.clone.1) | dynamic-update-slice | bytes 1179652 | tf_op jit(solution)/shard_map/dynamic_update_slice | solution.py:62
  418.1 2.6 fusion.39
  420.7 6.3 %dynamic_update_slice.29 = f32[50,26,128]{2,1,0:T(8,128)S(1)} dynamic-update-slice(f32[50,26,128]{2,1,0:T(8,128)S(1)} %dynamic_update_slice.28, f32[48,24,128]{2,1,0:T(8,128)} %fusion.39, s32[]{:T(128)} %constant.5.clone.1, s32[]{:T(128)} %constant.7.clone.1, s32[]{:T(128)} %constant.5.clone.1) | dynamic-update-slice | bytes 1179652 | tf_op jit(solution)/shard_map/dynamic_update_slice | solution.py:62
  427.0 1.9 fusion.45
  428.9 2.6 fusion.48
  431.5 6.3 %dynamic_update_slice.31 = f32[50,26,128]{2,1,0:T(8,128)S(1)} dynamic-update-slice(f32[50,26,128]{2,1,0:T(8,128)S(1)} %fusion.45, f32[48,24,128]{2,1,0:T(8,128)} %fusion.48, s32[]{:T(128)} %constant.6.clone.1, s32[]{:T(128)} %constant.6.clone.1, s32[]{:T(128)} %constant.5.clone.1) | dynamic-update-slice | bytes 1179652 | tf_op jit(solution)/shard_map/dynamic_update_slice | solution.py:62
  437.8 2.6 fusion.51
  440.4 6.3 %dynamic_update_slice.32 = f32[50,26,128]{2,1,0:T(8,128)S(1)} dynamic-update-slice(f32[50,26,128]{2,1,0:T(8,128)S(1)} %dynamic_update_slice.31, f32[48,24,128]{2,1,0:T(8,128)} %fusion.51, s32[]{:T(128)} %constant.6.clone.1, s32[]{:T(128)} %constant.7.clone.1, s32[]{:T(128)} %constant.5.clone.1) | dynamic-update-slice | bytes 1179652 | tf_op jit(solution)/shard_map/dynamic_update_slice | solution.py:62
  446.7 1.8 fusion.57
  448.5 2.6 fusion.60
  451.1 6.2 %dynamic_update_slice.34 = f32[50,26,128]{2,1,0:T(8,128)S(1)} dynamic-update-slice(f32[50,26,128]{2,1,0:T(8,128)S(1)} %fusion.57, f32[48,24,128]{2,1,0:T(8,128)} %fusion.60, s32[]{:T(128)} %constant.7.clone.1, s32[]{:T(128)} %constant.6.clone.1, s32[]{:T(128)} %constant.5.clone.1) | dynamic-update-slice | bytes 1179652 | tf_op jit(solution)/shard_map/dynamic_update_slice | solution.py:62
  457.3 2.6 fusion.63
  459.9 6.2 %dynamic_update_slice.35 = f32[50,26,128]{2,1,0:T(8,128)S(1)} dynamic-update-slice(f32[50,26,128]{2,1,0:T(8,128)S(1)} %dynamic_update_slice.34, f32[48,24,128]{2,1,0:T(8,128)} %fusion.63, s32[]{:T(128)} %constant.7.clone.1, s32[]{:T(128)} %constant.7.clone.1, s32[]{:T(128)} %constant.5.clone.1) | dynamic-update-slice | bytes 1179652 | tf_op jit(solution)/shard_map/dynamic_update_slice | solution.py:62
  466.1 0.8 fusion.120
  466.9 0.0 reduce-scatter.2.cloned.1.call-done
  466.9 1.8 convert_bitcast_fusion
  468.7 38.0 %collective-permute-done.4 = f32[1024,3,3,128]{3,0,2,1:T(8,128)} collective-permute-done((f32[1024,3,3,128]{3,0,2,1:T(8,128)}, f32[1024,3,3,128]{3,0,2,1:T(8,128)}, u32[]{:S(2)}, u32[]{:S(2)}) %collective-permute-start.4) | collective-permute-done | bytes 4718624 | tf_op jit(solution)/shard_map/ppermute | solution.py:12
  506.7 1.7 fusion.165
Async XLA Ops:
  7.2 48.3 %copy-start.1 = (bf16[1,48,24,128]{3,2,1,0:T(8,128)(2,1)S(1)}, bf16[1,48,24,128]{3,2,1,0:T(8,128)(2,1)}, u32[]{:S(2)}) copy-start(bf16[1,48,24,128]{3,2,1,0:T(8,128)(2,1)} %param.3) | copy-start | bytes 884740
  7.2 45.1 %all-gather.2.cloned.1.call-start = ((), (), s32[]{:S(2)}) async-start(), calls=%async_computation.2 | async-start | bytes 2654208 | tf_op jit(solution)/shard_map/all_gather | solution.py:53
  7.9 459.0 %reduce-scatter.2.cloned.1.call-start = ((), (), s32[]{:S(2)}) async-start(), calls=%async_computation.1 | async-start | bytes 5308416 | tf_op jit(solution)/shard_map/reduce_scatter | solution.py:44
  52.3 3.2 copy-start
  72.4 11.4 %collective-permute-start = (f32[1024,3,3,128]{3,0,2,1:T(8,128)}, f32[1024,3,3,128]{3,0,2,1:T(8,128)S(1)}, u32[]{:S(2)}, u32[]{:S(2)}) collective-permute-start(f32[1024,3,3,128]{3,0,2,1:T(8,128)} %copy.48), channel_id=1, source_target_pairs={{0,8},{8,0},{16,24},{24,16},{32,40},{40,32},{48,56},{56,48},{64,72... | collective-permute-start | bytes 14155784 | tf_op jit(solution)/shard_map/ppermute | solution.py:12
  86.9 108.4 %copy-start.2 = (bf16[3,3,128,1024]{3,2,1,0:T(8,128)(2,1)S(1)}, bf16[3,3,128,1024]{3,2,1,0:T(8,128)(2,1)}, u32[]{:S(2)}) copy-start(bf16[3,3,128,1024]{3,2,1,0:T(8,128)(2,1)} %param.4) | copy-start | bytes 7077892
  86.9 103.1 %collective-permute-start.1 = (f32[1024,3,3,128]{3,0,2,1:T(8,128)S(1)}, f32[1024,3,3,128]{3,0,2,1:T(8,128)S(1)}, u32[]{:S(2)}, u32[]{:S(2)}) collective-permute-start(f32[1024,3,3,128]{3,0,2,1:T(8,128)S(1)} %add.88), channel_id=1, source_target_pairs={{0,16},{8,24},{16,0},{24,8},{32,48},{40,56},{48,32},{56,40},{64,80... | collective-permute-start | bytes 14155784 | tf_op jit(solution)/shard_map/ppermute | solution.py:12
  192.6 103.9 %collective-permute-start.2 = (f32[1024,3,3,128]{3,0,2,1:T(8,128)}, f32[1024,3,3,128]{3,0,2,1:T(8,128)}, u32[]{:S(2)}, u32[]{:S(2)}) collective-permute-start(f32[1024,3,3,128]{3,0,2,1:T(8,128)} %add.89), channel_id=1, source_target_pairs={{0,32},{8,40},{16,48},{24,56},{32,0},{40,8},{48,16},{56,24},{64,96... | collective-permute-start | bytes 14155784 | tf_op jit(solution)/shard_map/ppermute | solution.py:12
  300.8 101.3 %collective-permute-start.3 = (f32[1024,3,3,128]{3,0,2,1:T(8,128)S(1)}, f32[1024,3,3,128]{3,0,2,1:T(8,128)S(1)}, u32[]{:S(2)}, u32[]{:S(2)}) collective-permute-start(f32[1024,3,3,128]{3,0,2,1:T(8,128)S(1)} %add.90), channel_id=1, source_target_pairs={{0,64},{8,72},{16,80},{24,88},{32,96},{40,104},{48,112},{56,120},{... | collective-permute-start | bytes 14155784 | tf_op jit(solution)/shard_map/ppermute | solution.py:12
  404.7 102.1 %collective-permute-start.4 = (f32[1024,3,3,128]{3,0,2,1:T(8,128)}, f32[1024,3,3,128]{3,0,2,1:T(8,128)}, u32[]{:S(2)}, u32[]{:S(2)}) collective-permute-start(f32[1024,3,3,128]{3,0,2,1:T(8,128)} %add.91), channel_id=1, source_target_pairs={{0,128},{8,136},{16,144},{24,152},{32,160},{40,168},{48,176},{56,1... | collective-permute-start | bytes 14155784 | tf_op jit(solution)/shard_map/ppermute | solution.py:12
Sparse Core Ops, SparseCore 0:
  9.8 42.4 all-gather.1
  227.2 57.9 reduce-scatter.1
